TPU v7x, 32 devices: a whole 2x2x4 slice. The times are simulated.
32 devices in a mesh: lev: 4 (over y, x), wave: 8 (over z, core).
Axes of the slice: x: 2, y: 2, z: 4, core: 2. Of those that a mesh axis runs over, the one named last changes fastest.
Arguments:
- vorticity: float32 [2, 32, 640, 640], P(None, 'lev', 'wave'), may hold values from -6 to 6
- wind_lam: float32 [32, 640, 1280], P('lev', 'wave'), may hold values from -6 to 6
- wind_mu: float32 [32, 640, 1280], P('lev', 'wave'), may hold values from -6 to 6
- modes: float32 [32, 32], replicated, may hold values from -0.5 to 1.5, as said below
- mode_rates: float32 [32], replicated, may hold values from 0.05 to 2
- wave_order: int32 [640], replicated, may hold values from 0 to 639, each once
- lat_order: int32 [640], replicated, may hold values from 0 to 639, each once
Outputs:
- advanced: float32 [2, 32, 640, 640], P(None, 'lev', 'wave')
- stream: float32 [2, 32, 640, 640], P(None, 'lev', 'wave')
Inputs may be any that keep to these rules, and one draw needn't show every extreme that they name: `wave_order`: A permutation: each wavenumber 0 to 639 is held by exactly one slot. `lat_order`: A permutation: each latitude 0 to 639 is held by exactly one slot. `modes`: A dense real matrix.
All inputs are finite; a program needn't handle non-finite values.
Results may differ from a plain program's by a relative error of at most 0.0003.
Values sent between devices are 32-bit elements; how exact they have to be, the bound alone decides.
A program may use at most 320 MiB of HBM per device.

v0:
```python
import math

import jax
import jax.numpy as jnp
from jax import lax
from jax.sharding import PartitionSpec as P

M = 640
LAT = 640
GRID_LONGITUDES = 1280


HIGH_ACCURACY = lax.Precision.HIGHEST
TIME_STEP = 0.4


def latitudes(lat_order):
    angles = math.pi * (lat_order.astype(jnp.float32) + 0.75) / (LAT + 0.5)
    sines = jnp.sin(angles)
    return (jnp.cos(angles), sines, math.pi / (LAT + 0.5) * sines)


def legendre(waves, cosines, sines, degrees):
    wavenum = waves.astype(jnp.float32)[:, None]
    counter = jnp.arange(1, M, dtype=jnp.int32).astype(jnp.float32)
    halves = 0.5 * jnp.log((2.0 * counter + 1.0) / (2.0 * counter))
    start_log = jnp.sum(jnp.where(counter[None, :] <= wavenum, halves[None, :], 0.0), axis=1)
    log_start = -0.5 * math.log(2.0) + start_log[:, None] + wavenum * jnp.log(sines)[None, :]

    def advance(carry, step_index):
        previous, current, log_scale = carry
        emitted = current * jnp.exp(log_scale)
        degree = wavenum + step_index.astype(jnp.float32) + 1.0
        factor_ahead = jnp.sqrt(
            (4.0 * degree * degree - 1.0) / (degree * degree - wavenum * wavenum)
        )
        lower_degree = degree - 1.0
        factor_behind = jnp.sqrt(
            (lower_degree * lower_degree - wavenum * wavenum)
            / (4.0 * lower_degree * lower_degree - 1.0)
        )
        following = factor_ahead * (cosines[None, :] * current - factor_behind * previous)
        magnitude = jnp.abs(current) + jnp.abs(following)
        return (
            (current / magnitude, following / magnitude, log_scale + jnp.log(magnitude)),
            emitted,
        )

    initial = (
        jnp.zeros(log_start.shape, jnp.float32),
        jnp.ones(log_start.shape, jnp.float32),
        log_start,
    )
    last_carry, stacked = lax.scan(
        advance, initial, jnp.arange(degrees, dtype=jnp.int32), unroll=32
    )
    live_mask = (waves[:, None] + jnp.arange(degrees, dtype=jnp.int32)[None, :] < M).astype(
        jnp.float32
    )
    return jnp.transpose(stacked, (1, 0, 2)) * live_mask[:, :, None]


def coupling(waves):
    wavenum = waves.astype(jnp.float32)[:, None]
    degree = wavenum + jnp.arange(M, dtype=jnp.int32).astype(jnp.float32)[None, :]
    live_mask = (degree < M - 0.5).astype(jnp.float32)
    square = wavenum * wavenum
    eps_here = jnp.sqrt((degree * degree - square) / (4.0 * degree * degree - 1.0))
    degree_next = degree + 1.0
    eps_ahead = jnp.sqrt(
        (degree_next * degree_next - square) / (4.0 * degree_next * degree_next - 1.0)
    )
    kappa = degree * (degree + 1.0) / (M * (M + 1.0))
    return (
        -(degree - 1.0) * eps_here * live_mask,
        (degree + 2.0) * eps_ahead * live_mask,
        live_mask,
        kappa,
    )


def fourier(waves):
    phase = waves[:, None] * jnp.arange(GRID_LONGITUDES, dtype=jnp.int32)[None, :] % GRID_LONGITUDES
    angles = 2.0 * math.pi / GRID_LONGITUDES * phase.astype(jnp.float32)
    return jnp.concatenate([jnp.cos(angles), jnp.sin(angles)], axis=0)


def lowered(spectra):
    return jnp.concatenate([jnp.zeros_like(spectra[..., :1]), spectra[..., :-1]], axis=-1)


def raised(spectra):
    return jnp.concatenate([spectra[..., 1:], jnp.zeros_like(spectra[..., :1])], axis=-1)


def on_device(vorticity, wind_lam, wind_mu, modes, mode_rates, wave_order, lat_order):
    slots = vorticity.shape[2]
    wave_pos = lax.axis_index("wave")
    lev_pos = lax.axis_index("lev")
    waves = lax.dynamic_slice_in_dim(wave_order, wave_pos * slots, slots)
    cosines, sines, weights = latitudes(lat_order)
    legendre_table = legendre(waves, cosines, sines, M)
    lower, upper, live_mask, kappa = coupling(waves)
    trigonometric_table = fourier(wave_order)
    double = jnp.where(wave_order == 0, 1.0, 2.0).astype(jnp.float32)
    scaled = double * wave_order.astype(jnp.float32)

    def tendency(spectra):
        meridional = lower * lowered(spectra) + upper * raised(spectra)
        both = jnp.stack([spectra, meridional])
        at_lat = jnp.einsum("fclsj,sjr->fclsr", both, legendre_table, precision=HIGH_ACCURACY)
        at_lat = lax.all_to_all(at_lat, "wave", split_axis=4, concat_axis=3, tiled=True)
        zonal = jnp.concatenate(
            [-(scaled[:, None] * at_lat[0, 1]), -(scaled[:, None] * at_lat[0, 0])], axis=1
        )
        merid = jnp.concatenate(
            [double[:, None] * at_lat[1, 0], -(double[:, None] * at_lat[1, 1])], axis=1
        )
        grid = jnp.einsum(
            "flsr,sk->flrk", jnp.stack([zonal, merid]), trigonometric_table, precision=HIGH_ACCURACY
        )
        source_term = -(wind_lam * grid[0] + wind_mu * grid[1])
        spectral_latitude_fields = (
            jnp.einsum("nqy,zy->nzq", source_term, trigonometric_table, precision=HIGH_ACCURACY)
            / GRID_LONGITUDES
        )
        returned = jnp.stack([spectral_latitude_fields[:, :M], -spectral_latitude_fields[:, M:]])
        returned = (
            lax.all_to_all(returned, "wave", split_axis=2, concat_axis=3, tiled=True) * weights
        )
        return jnp.einsum("clsr,sjr->clsj", returned, legendre_table, precision=HIGH_ACCURACY)

    start = vorticity * live_mask
    first_rate = tendency(start)
    middle = start + TIME_STEP / M * first_rate
    second_rate = tendency(middle)
    advanced = start + 0.5 * TIME_STEP / M * (first_rate + second_rate)
    regrouped_fields = lax.all_to_all(advanced, "lev", split_axis=3, concat_axis=1, tiled=True)
    block_width = regrouped_fields.shape[3]
    diffusion_block = lax.dynamic_slice_in_dim(kappa, lev_pos * block_width, block_width, 1)
    projected = jnp.einsum("lk,clsj->cksj", modes, regrouped_fields, precision=HIGH_ACCURACY)
    projected = projected / (diffusion_block[None, None] + mode_rates[None, :, None, None])
    restored = jnp.einsum("lk,cksj->clsj", modes, projected, precision=HIGH_ACCURACY)
    stream = lax.all_to_all(restored, "lev", split_axis=1, concat_axis=3, tiled=True)
    stream = stream * live_mask
    return (advanced, stream)


def solution(mesh):
    placed = (
        P(None, "lev", "wave", None),
        P("lev", "wave", None),
        P("lev", "wave", None),
        P(),
        P(),
        P(),
        P(),
    )
    return jax.shard_map(
        on_device,
        mesh=mesh,
        in_specs=placed,
        out_specs=(P(None, "lev", "wave", None), P(None, "lev", "wave", None)),
        check_vma=False,
    )
```

profile of v0, /device:TPU:0, one launch (start us, length us, event | category | flops | bytes accessed | tf_op | source)
XLA Modules:
  0.0 2306.6 jit_solution(1412973736084589304)
XLA Ops:
  11.2 661.5 %while.22 = (s32[]{:T(128)}, f32[80,640]{1,0:T(8,128)S(1)}, f32[80,640]{1,0:T(8,128)S(1)}, f32[80,640]{1,0:T(8,128)S(1)}, f32[20,32,80,640]{3,2,1,0:T(8,128)}, /...) while((s32[]{:T(128)}, f32[80,640]{1,0:T(8,128)S(1)}, ...), condition=%wide.region_2.3_spmd.clone, body=%wide.region_1.2_spmd.clone.sunk | while | flops 30653472 | bytes 65111436 | solution.py:54
  679.2 110.6 %fusion.310 = f32[2,2,8,80,640]{4,2,1,0,3:T(8,128)} fusion(f32[640,80,640]{2,1,0:T(8,128)} %bitcast.2, f32[80,640]{1,0:T(8,128)S(1)} %fusion.355, f32[2,2,8,80,640]{4,2,1,0,3:T(8,128)S(1)} %fusion.394), kind=kOutput, calls=%fused_computation.616 | convolution fusion | flops 12615680000 | bytes 144384000 | tf_op jit(solution)/shard_map/fclsj,sjr->fclsr/dot_general | solution.py:111
  789.8 10.1 copy.96
  806.6 14.8 fusion.308
  821.4 214.0 %all-to-all-done = f32[2,2,8,80,640]{3,2,1,0,4:T(8,128)} async-done(((f32[2,2,8,80,640]{3,2,1,0,4:T(8,128)}), f32[2,2,8,80,640]{3,2,1,0,4:T(8,128)}, u32[]{:S(2)}, u32[]{:S(2)}) %all-to-all-start) | async-done | bytes 6553632 | tf_op jit(solution)/shard_map/all_to_all | solution.py:112
  1035.4 14.0 copy.169
  1049.4 10.0 all_to_all.81
  1064.8 29.6 %fusion.255 = f32[2,8,80,1280]{3,2,1,0:T(8,128)} fusion(f32[1,8,1280,80]{2,3,1,0:T(8,128)S(1)} %get-tuple-element.681, f32[1,8,1280,80]{2,3,1,0:T(8,128)S(1)} %get-tuple-element.680, f32[640,1280]{1,0:T(8,128)S(1)} %copy-done.4, f32[640,1280]{1,0:T(8,128)S(1)} %get-tuple-element.671), kind=kOutput, calls=%fused_computation.551 | convolution fusion | flops 25169100800 | bytes 19660800 | tf_op jit(solution)/shard_map/flsr,sk->flrk/dot_general | solution.py:119
  1094.5 16.8 fusion.283
  1115.7 120.1 %all_to_all.108 = f32[2,8,640,80]{3,1,0,2:T(8,128)S(1)} all-to-all(f32[2,8,640,80]{3,1,0,2:T(8,128)} %copy.98), channel_id=1, replica_groups=mesh['lev'=4,'wave'=8] {'wave'}, dimensions={2} | all-to-all | bytes 6553600 | tf_op jit(solution)/shard_map/all_to_all | solution.py:129
  1249.4 155.2 %bitcast_add_fusion.34 = (f32[2,8,80,640]{3,1,0,2:T(8,128)S(1)}, f32[80,640,16]{1,2,0}) fusion(f32[2,8,80,640]{3,1,0,2:T(8,128)S(1)} %copy-done.1, f32[640,80,640]{2,1,0:T(8,128)} %bitcast.2, f32[80,640]{1,0:T(8,128)S(1)} %fusion.355, f32[80,640,16]{1,2,0:T(8,128)S(1)} %fusion.301.clone.5), kind=kOutput, calls=%fused_computation.603 | convolution fusion | flops 6325862400 | bytes 144384000
  1409.8 109.9 %fusion.315 = f32[2,2,8,80,640]{4,2,1,0,3:T(8,128)} fusion(f32[640,80,640]{2,1,0:T(8,128)} %bitcast.2, f32[80,640]{1,0:T(8,128)S(1)} %fusion.355, f32[2,2,8,80,640]{4,2,1,0,3:T(8,128)} %fusion.396), kind=kOutput, calls=%fused_computation.617 | convolution fusion | flops 12615680000 | bytes 144384000 | tf_op jit(solution)/shard_map/fclsj,sjr->fclsr/dot_general | solution.py:111
  1519.7 10.1 copy.101
  1529.8 232.8 %all_to_all.109 = f32[2,2,8,80,640]{3,2,1,0,4:T(8,128)S(1)} all-to-all(f32[2,2,8,80,640]{3,2,1,0,4:T(8,128)} %copy.101), channel_id=1, replica_groups=mesh['lev'=4,'wave'=8] {'wave'}, dimensions={4} | all-to-all | bytes 13107200 | tf_op jit(solution)/shard_map/all_to_all | solution.py:112
  1762.7 9.9 copy.168
  1772.6 10.1 all_to_all.89
  1789.3 28.3 %fusion.259 = f32[2,8,80,1280]{3,2,1,0:T(8,128)S(1)} fusion(f32[1,8,1280,80]{2,3,1,0:T(8,128)S(1)} %maximum_bitcast_fusion.3, f32[1,8,1280,80]{2,3,1,0:T(8,128)S(1)} %maximum_bitcast_fusion.2, f32[640,1280]{1,0:T(8,128)S(1)} %copy-done.5, f32[640,1280]{1,0:T(8,128)S(1)} %copy-done.3), kind=kOutput, calls=%fused_computation.556 | convolution fusion | flops 25169100800 | bytes 19660800 | tf_op jit(solution)/shard_map/flsr,sk->flrk/dot_general | solution.py:119
  1817.6 14.7 fusion.280
  1840.1 120.1 %all_to_all.110 = f32[2,8,640,80]{3,1,0,2:T(8,128)S(1)} all-to-all(f32[2,8,640,80]{3,1,0,2:T(8,128)} %copy.103), channel_id=1, replica_groups=mesh['lev'=4,'wave'=8] {'wave'}, dimensions={2} | all-to-all | bytes 6553600 | tf_op jit(solution)/shard_map/all_to_all | solution.py:129
  1973.8 155.0 %bitcast_add_fusion.32 = f32[2,8,80,640]{3,1,0,2:T(8,128)} fusion(f32[2,8,80,640]{3,1,0,2:T(8,128)S(1)} %copy-done.1, f32[80,640,16]{1,2,0:S(1)} %copy-done.13, f32[640,80,640]{2,1,0:T(8,128)} %bitcast.2, f32[80,640]{1,0:T(8,128)S(1)} %fusion.355, f32[80,640,16]{1,2,0:T(8,128)S(1)} %fusion.391), kind=kOutput, calls=%fused_computation.600 | convolution fusion | flops 6326681600 | bytes 144384000
  2141.1 57.0 %all-to-all-done.4 = f32[2,8,80,640]{2,1,0,3:T(8,128)} async-done(((f32[2,8,80,640]{2,1,0,3:T(8,128)}), f32[2,8,80,640]{2,1,0,3:T(8,128)}, u32[]{:S(2)}, u32[]{:S(2)}) %all-to-all-start.4) | async-done | bytes 3276832 | tf_op jit(solution)/shard_map/all_to_all | solution.py:138
  2205.3 10.1 fusion.271
  2234.4 55.4 %all-to-all-done.5 = f32[2,32,80,160]{3,2,0,1:T(8,128)} async-done(((f32[2,32,80,160]{3,2,0,1:T(8,128)}), f32[2,32,80,160]{3,2,0,1:T(8,128)}, u32[]{:S(2)}, u32[]{:S(2)}) %all-to-all-start.5) | async-done | bytes 3276832 | tf_op jit(solution)/shard_map/all_to_all | solution.py:144
  2289.9 8.2 copy.170
  (903 shorter events, 388.2 us)
Async XLA Ops:
  0.6 2204.7 %copy-start = (f32[32,32]{1,0:T(8,128)S(1)}, f32[32,32]{1,0:T(8,128)}, u32[]{:S(2)}) copy-start(f32[32,32]{1,0:T(8,128)} %param.12) | copy-start | bytes 12292
  1.7 4.9 copy-start.14
  1.7 4.9 copy-start.11
  6.6 2.8 copy-start.22
  11.2 665.5 %copy-start.16 = (f32[80,640]{1,0:T(8,128)}, f32[80,640]{1,0:T(8,128)S(1)}, u32[]{:S(2)}) copy-start(f32[80,640]{1,0:T(8,128)S(1)} %get-tuple-element.666) | copy-start | bytes 614404
  11.2 665.5 %copy-start.18 = (f32[80,640]{1,0:T(8,128)}, f32[80,640]{1,0:T(8,128)S(1)}, u32[]{:S(2)}) copy-start(f32[80,640]{1,0:T(8,128)S(1)} %get-tuple-element.667) | copy-start | bytes 614404
  676.7 1.9 copy-start.12
  799.8 6.7 copy-start.21
  799.8 235.6 %all-to-all-start = ((f32[2,2,8,80,640]{3,2,1,0,4:T(8,128)}), f32[2,2,8,80,640]{3,2,1,0,4:T(8,128)}, u32[]{:S(2)}, u32[]{:S(2)}) async-start(f32[2,2,8,80,640]{3,2,1,0,4:T(8,128)} %copy.96), calls=%async_computation | async-start | bytes 20971520 | tf_op jit(solution)/shard_map/all_to_all | solution.py:112
  821.4 273.1 %copy-start.2 = (f32[640,1280]{1,0:T(8,128)}, f32[640,1280]{1,0:T(8,128)S(1)}, u32[]{:S(2)}) copy-start(f32[640,1280]{1,0:T(8,128)S(1)} %get-tuple-element.671) | copy-start | bytes 9830404
  1062.9 1.9 copy-start.4
  1064.8 29.6 %copy-start.7 = (f32[8,80,1280]{2,1,0:T(8,128)S(1)}, f32[8,80,1280]{2,1,0:T(8,128)}, u32[]{:S(2)}) copy-start(f32[8,80,1280]{2,1,0:T(8,128)} %param.11) | copy-start | bytes 9830404
  1064.8 29.7 %copy-start.9 = (f32[8,80,1280]{2,1,0:T(8,128)S(1)}, f32[8,80,1280]{2,1,0:T(8,128)}, u32[]{:S(2)}) copy-start(f32[8,80,1280]{2,1,0:T(8,128)} %param.10) | copy-start | bytes 9830404
  1241.1 5.4 copy-start.20
  1246.5 2.9 copy-start.1
  1786.4 2.9 copy-start.5
  1789.3 28.3 %copy-start.8 = (f32[8,80,1280]{2,1,0:T(8,128)S(1)}, f32[8,80,1280]{2,1,0:T(8,128)}, u32[]{:S(2)}) copy-start(f32[8,80,1280]{2,1,0:T(8,128)} %param.11) | copy-start | bytes 9830404
  1789.3 28.3 %copy-start.10 = (f32[8,80,1280]{2,1,0:T(8,128)S(1)}, f32[8,80,1280]{2,1,0:T(8,128)}, u32[]{:S(2)}) copy-start(f32[8,80,1280]{2,1,0:T(8,128)} %param.10) | copy-start | bytes 9830404
  1970.9 2.9 copy-start.13
  2134.4 6.3 copy-start.23
  2134.4 63.7 %all-to-all-start.4 = ((f32[2,8,80,640]{2,1,0,3:T(8,128)}), f32[2,8,80,640]{2,1,0,3:T(8,128)}, u32[]{:S(2)}, u32[]{:S(2)}) async-start(f32[2,8,80,640]{2,1,0,3:T(8,128)} %copy.105), calls=%async_computation.4 | async-start | bytes 10485760 | tf_op jit(solution)/shard_map/all_to_all | solution.py:138
  2226.2 5.5 copy-start.6
  2226.2 63.6 %all-to-all-start.5 = ((f32[2,32,80,160]{3,2,0,1:T(8,128)}), f32[2,32,80,160]{3,2,0,1:T(8,128)}, u32[]{:S(2)}, u32[]{:S(2)}) async-start(f32[2,32,80,160]{3,2,0,1:T(8,128)} %copy.110), calls=%async_computation.5 | async-start | bytes 10485760 | tf_op jit(solution)/shard_map/all_to_all | solution.py:144
  2298.1 5.3 copy-start.15
  (3 other events, 4.1 us)
where the time goes:
time: 2320 us; the launch traced here: 2310 us
  matrix products  636 us (27%)
  blocking collectives  473 us (20%)
  loops' own time  400 us (17%)
  waiting for transfers between devices  326 us (14%)
  local copies, waits for them, and re-layouts  235 us (10%)
  other arithmetic  218 us (9%)
    another operation x1, loops' own time, legendre(): lax.scan(advance, initial, jnp.arange(degrees, dtype=jnp.int32), unroll=32)  400 us
    unnamed x2, matrix products  310 us
    all_to_all x2, blocking collectives, tendency(): lax.all_to_all(returned, 'wave', split_axis=2, concat_axis=3, tiled=True)  240 us
    all_to_all x1, blocking collectives, tendency(): lax.all_to_all(at_lat, 'wave', split_axis=4, concat_axis=3, tiled=True)  233 us
    dot_general x2, matrix products, tendency(): jnp.einsum('fclsj,sjr->fclsr', both, legendre_table, precision=HIGH_ACCUR...  221 us
    all_to_all x1, waiting for transfers between devices, tendency(): lax.all_to_all(at_lat, 'wave', split_axis=4, concat_axis=3, tiled=True)  214 us
    while x620, other arithmetic  155 us
    dynamic_update_slice x20, local copies, waits for them, and re-layouts, legendre(): lax.scan(advance, initial, jnp.arange(degrees, dtype=jnp.int32), unroll=32)  62.9 us
  transfers between devices with their start and end apart: 3, of which 3 were waited for; matrix products, arithmetic and copies ran while one was open for 1% of the time, Pallas kernels for 0%

commit v1 on v0

--- a/solution.py
+++ b/solution.py
@@ -1,8 +1,11 @@
+import functools
 import math
 
 import jax
 import jax.numpy as jnp
 from jax import lax
+from jax.experimental import pallas as pl
+from jax.experimental.pallas import tpu as pltpu
 from jax.sharding import PartitionSpec as P
 
 M = 640
@@ -10,7 +13,7 @@
 GRID_LONGITUDES = 1280
 
 
-HIGH_ACCURACY = lax.Precision.HIGHEST
+HIGH_ACCURACY = lax.Precision.HIGH
 TIME_STEP = 0.4
 
 
@@ -18,6 +21,46 @@
     angles = math.pi * (lat_order.astype(jnp.float32) + 0.75) / (LAT + 0.5)
     sines = jnp.sin(angles)
     return (jnp.cos(angles), sines, math.pi / (LAT + 0.5) * sines)
+
+
+GROUP = 8
+LANES = 128
+VMEM = 60 * 1024 * 1024
+
+
+def table_kernel(ahead_ref, behind_ref, start_ref, cos_ref, out_ref):
+    lats = out_ref.shape[2]
+    spans = [(k, min(LANES, lats - k)) for k in range(0, lats, LANES)]
+    mus = [jnp.broadcast_to(cos_ref[0:1, k : k + n], (GROUP, n)) for k, n in spans]
+
+    def block(index, carry):
+        first = pl.multiple_of(index * 8, 8)
+        ahead = [ahead_ref[first + t] for t in range(8)]
+        behind = [behind_ref[first + t] for t in range(8)]
+        following_carry = []
+        for (k, n), mu, (previous, current, log_scale) in zip(spans, mus, carry):
+            scale = jnp.exp(log_scale)
+            rows = []
+            for t in range(8):
+                rows.append(current * scale)
+                following = ahead[t][:, :n] * (mu * current - behind[t][:, :n] * previous)
+                previous, current = current, following
+            magnitude = jnp.abs(previous) + jnp.abs(current)
+            following_carry.append(
+                (previous / magnitude, current / magnitude, log_scale + jnp.log(magnitude))
+            )
+            out_ref[:, pl.ds(first, 8), k : k + n] = jnp.swapaxes(jnp.stack(rows), 0, 1)
+        return tuple(following_carry)
+
+    initial = tuple(
+        (
+            jnp.zeros((GROUP, n), jnp.float32),
+            jnp.ones((GROUP, n), jnp.float32),
+            start_ref[:, k : k + n],
+        )
+        for k, n in spans
+    )
+    lax.fori_loop(0, out_ref.shape[1] // 8, block, initial)
 
 
 def legendre(waves, cosines, sines, degrees):
@@ -26,38 +69,114 @@
     halves = 0.5 * jnp.log((2.0 * counter + 1.0) / (2.0 * counter))
     start_log = jnp.sum(jnp.where(counter[None, :] <= wavenum, halves[None, :], 0.0), axis=1)
     log_start = -0.5 * math.log(2.0) + start_log[:, None] + wavenum * jnp.log(sines)[None, :]
-
-    def advance(carry, step_index):
-        previous, current, log_scale = carry
-        emitted = current * jnp.exp(log_scale)
-        degree = wavenum + step_index.astype(jnp.float32) + 1.0
-        factor_ahead = jnp.sqrt(
-            (4.0 * degree * degree - 1.0) / (degree * degree - wavenum * wavenum)
-        )
-        lower_degree = degree - 1.0
-        factor_behind = jnp.sqrt(
-            (lower_degree * lower_degree - wavenum * wavenum)
-            / (4.0 * lower_degree * lower_degree - 1.0)
-        )
-        following = factor_ahead * (cosines[None, :] * current - factor_behind * previous)
-        magnitude = jnp.abs(current) + jnp.abs(following)
-        return (
-            (current / magnitude, following / magnitude, log_scale + jnp.log(magnitude)),
-            emitted,
-        )
-
-    initial = (
-        jnp.zeros(log_start.shape, jnp.float32),
-        jnp.ones(log_start.shape, jnp.float32),
+    degree = wavenum.T + jnp.arange(degrees, dtype=jnp.int32).astype(jnp.float32)[:, None] + 1.0
+    square = wavenum.T * wavenum.T
+    ahead = jnp.sqrt((4.0 * degree * degree - 1.0) / (degree * degree - square))
+    lower = degree - 1.0
+    behind = jnp.sqrt((lower * lower - square) / (4.0 * lower * lower - 1.0))
+    slots, lats = waves.shape[0], cosines.shape[0]
+    wide = (degrees, slots, LANES)
+    coefficient = pl.BlockSpec((degrees, GROUP, LANES), lambda g: (0, g, 0))
+    return pl.pallas_call(
+        table_kernel,
+        grid=(slots // GROUP,),
+        in_specs=[
+            coefficient,
+            coefficient,
+            pl.BlockSpec((GROUP, lats), lambda g: (g, 0)),
+            pl.BlockSpec((1, lats), lambda g: (0, 0)),
+        ],
+        out_specs=pl.BlockSpec((GROUP, degrees, lats), lambda g: (g, 0, 0)),
+        out_shape=jax.ShapeDtypeStruct((slots, degrees, lats), jnp.float32),
+        compiler_params=pltpu.CompilerParams(vmem_limit_bytes=VMEM),
+        name="table",
+    )(
+        jnp.broadcast_to(ahead[:, :, None], wide),
+        jnp.broadcast_to(behind[:, :, None], wide),
         log_start,
-    )
-    last_carry, stacked = lax.scan(
-        advance, initial, jnp.arange(degrees, dtype=jnp.int32), unroll=32
-    )
-    live_mask = (waves[:, None] + jnp.arange(degrees, dtype=jnp.int32)[None, :] < M).astype(
-        jnp.float32
-    )
-    return jnp.transpose(stacked, (1, 0, 2)) * live_mask[:, :, None]
+        cosines[None, :],
+    )
+
+
+def halves_of(value):
+    high = value.astype(jnp.bfloat16)
+    return high, (value - high.astype(jnp.float32)).astype(jnp.bfloat16)
+
+
+def three_products(fields, table, contract):
+    rows = fields.shape[0]
+    field_high, field_low = halves_of(fields)
+    table_high, table_low = halves_of(table)
+    dims = (((1,), (contract,)), ((), ()))
+    both = lax.dot_general(
+        jnp.concatenate([field_high, field_low], axis=0),
+        table_high,
+        dims,
+        preferred_element_type=jnp.float32,
+    )
+    small = lax.dot_general(field_high, table_low, dims, preferred_element_type=jnp.float32)
+    return both[:rows] + (both[rows:] + small)
+
+
+def transform_kernel(waves_ref, fields_ref, table_ref, out_ref, turned, result, *, forward):
+    degrees = table_ref.shape[1]
+    turned[...] = jnp.swapaxes(fields_ref[...], 0, 1)
+    group = pl.program_id(0)
+    for i in range(GROUP):
+        alive = degrees - waves_ref[group * GROUP + i]
+        for first in range(0, degrees, 256):
+            last = min(first + 256, degrees)
+
+            @pl.when(alive > first)
+            def _():
+                table = table_ref[i, first:last, :]
+                if forward:
+                    result[i, :, first:last] = three_products(turned[i], table, 1)
+                elif first == 0:
+                    result[i] = three_products(turned[i, :, first:last], table, 0)
+                else:
+                    result[i] += three_products(turned[i, :, first:last], table, 0)
+
+            if forward:
+
+                @pl.when(alive <= first)
+                def _():
+                    result[i, :, first:last] = jnp.zeros(
+                        (result.shape[1], last - first), jnp.float32
+                    )
+
+    out_ref[...] = jnp.swapaxes(result[...], 0, 1)
+
+
+def transform(waves, fields, table, forward):
+    rows, slots, width = fields.shape
+    degrees, lats = table.shape[1:]
+    out_width = degrees if forward else lats
+    return pl.pallas_call(
+        functools.partial(transform_kernel, forward=forward),
+        grid_spec=pltpu.PrefetchScalarGridSpec(
+            num_scalar_prefetch=1,
+            grid=(slots // GROUP,),
+            in_specs=[
+                pl.BlockSpec((rows, GROUP, width), lambda g, w: (0, g, 0)),
+                pl.BlockSpec((GROUP, degrees, lats), lambda g, w: (g, 0, 0)),
+            ],
+            out_specs=pl.BlockSpec((rows, GROUP, out_width), lambda g, w: (0, g, 0)),
+            scratch_shapes=[
+                pltpu.VMEM((GROUP, rows, width), jnp.float32),
+                pltpu.VMEM((GROUP, rows, out_width), jnp.float32),
+            ],
+        ),
+        out_shape=jax.ShapeDtypeStruct((rows, slots, out_width), jnp.float32),
+        compiler_params=pltpu.CompilerParams(vmem_limit_bytes=VMEM),
+        name="analysis" if forward else "synthesis",
+    )(waves, fields, table)
+
+
+def padded(array, axis, size):
+    widths = [(0, 0)] * array.ndim
+    widths[axis] = (0, size - array.shape[axis])
+    return jnp.pad(array, widths) if size > array.shape[axis] else array
 
 
 def coupling(waves):
@@ -99,7 +218,9 @@
     lev_pos = lax.axis_index("lev")
     waves = lax.dynamic_slice_in_dim(wave_order, wave_pos * slots, slots)
     cosines, sines, weights = latitudes(lat_order)
-    legendre_table = legendre(waves, cosines, sines, M)
+    full = -(-slots // GROUP) * GROUP
+    full_waves = padded(waves, 0, full)
+    legendre_table = legendre(full_waves, cosines, sines, M)
     lower, upper, live_mask, kappa = coupling(waves)
     trigonometric_table = fourier(wave_order)
     double = jnp.where(wave_order == 0, 1.0, 2.0).astype(jnp.float32)
@@ -108,7 +229,10 @@
     def tendency(spectra):
         meridional = lower * lowered(spectra) + upper * raised(spectra)
         both = jnp.stack([spectra, meridional])
-        at_lat = jnp.einsum("fclsj,sjr->fclsr", both, legendre_table, precision=HIGH_ACCURACY)
+        rows = both.shape[0] * both.shape[1] * both.shape[2]
+        flat = padded(both.reshape(rows, slots, M), 1, full)
+        at_lat = transform(full_waves, flat, legendre_table, False)[:, :slots]
+        at_lat = at_lat.reshape(both.shape[:4] + (LAT,))
         at_lat = lax.all_to_all(at_lat, "wave", split_axis=4, concat_axis=3, tiled=True)
         zonal = jnp.concatenate(
             [-(scaled[:, None] * at_lat[0, 1]), -(scaled[:, None] * at_lat[0, 0])], axis=1
@@ -128,7 +252,9 @@
         returned = (
             lax.all_to_all(returned, "wave", split_axis=2, concat_axis=3, tiled=True) * weights
         )
-        return jnp.einsum("clsr,sjr->clsj", returned, legendre_table, precision=HIGH_ACCURACY)
+        flat = padded(returned.reshape(rows // 2, slots, LAT), 1, full)
+        result = transform(full_waves, flat, legendre_table, True)[:, :slots]
+        return result.reshape(spectra.shape) * live_mask
 
     start = vorticity * live_mask
     first_rate = tendency(start)

time: 2320 us -> 1440 us (0.62)
  matrix products: 636 us -> 61.3 us
  loops' own time: 400 us -> 0 us
  Pallas kernels: 0 us -> 275 us
  other arithmetic: 218 us -> 79.5 us
  local copies, waits for them, and re-layouts: 235 us -> 197 us
    another operation x1 -> x0, loops' own time: 400 us -> none  [legendre(): lax.scan(advance, initial, jnp.arange(degrees, dtype=jnp.int32), unroll=32)]
    unnamed x2 -> x0, matrix products: 310 us -> none
    pallas_call x0 -> x5, Pallas kernels: none -> 275 us  [the longest x4 202 us: transform(): pl.pallas_call(functools.partial(transform_kernel, forward=forward), grid...]
    dot_general x2 -> x0, matrix products: 221 us -> none  [tendency(): jnp.einsum('fclsj,sjr->fclsr', both, legendre_table, precision=HIGH_ACCUR...]
    while x620 -> x0, other arithmetic: 155 us -> none
    dynamic_update_slice x20 -> x0, local copies, waits for them, and re-layouts: 62.9 us -> none  [legendre(): lax.scan(advance, initial, jnp.arange(degrees, dtype=jnp.int32), unroll=32)]
    reshape x0 -> x4, local copies, waits for them, and re-layouts: none -> 31.6 us  [the longest x2 20.2 us: tendency(): at_lat = at_lat.reshape(both.shape[:4] + (LAT,))]
    slice x40 -> x0, local copies, waits for them, and re-layouts: 28.5 us -> none  [legendre(): lax.scan(advance, initial, jnp.arange(degrees, dtype=jnp.int32), unroll=32)]
  transfers between devices with their start and end apart: 3 -> 3, of which waited for: 3 -> 3; matrix products, arithmetic and copies ran while one was open for 1% -> 2% of each run, Pallas kernels for 0% -> 0%
where the time goes in v1:
time: 1440 us; the launch traced here: 1430 us
  blocking collectives  476 us (33%)
  waiting for transfers between devices  323 us (22%)
  Pallas kernels  275 us (19%)
  local copies, waits for them, and re-layouts  197 us (14%)
  other arithmetic  79.5 us (6%)
  matrix products  61.3 us (4%)
  starting transfers between devices  18.9 us (1%)
    all_to_all x2, blocking collectives, tendency(): lax.all_to_all(returned, 'wave', split_axis=2, concat_axis=3, tiled=True)  241 us
    all_to_all x1, blocking collectives, tendency(): lax.all_to_all(at_lat, 'wave', split_axis=4, concat_axis=3, tiled=True)  235 us
    all_to_all x1, waiting for transfers between devices, tendency(): lax.all_to_all(at_lat, 'wave', split_axis=4, concat_axis=3, tiled=True)  214 us
    pallas_call x4, Pallas kernels, transform(): pl.pallas_call(functools.partial(transform_kernel, forward=forward), grid...  202 us
    pallas_call x1, Pallas kernels, legendre(): pl.pallas_call(table_kernel, grid=(slots // GROUP,), in_specs=[coefficien...  72.6 us
    all_to_all x1, waiting for transfers between devices, on_device(): lax.all_to_all(advanced, 'lev', split_axis=3, concat_axis=1, tiled=True)  56.8 us
    all_to_all x1, waiting for transfers between devices, on_device(): lax.all_to_all(restored, 'lev', split_axis=1, concat_axis=3, tiled=True)  52.5 us
    all_to_all x4, local copies, waits for them, and re-layouts, tendency(): lax.all_to_all(at_lat, 'wave', split_axis=4, concat_axis=3, tiled=True)  44 us
  transfers between devices with their start and end apart: 3, of which 3 were waited for; matrix products, arithmetic and copies ran while one was open for 2% of the time, Pallas kernels for 0%

profile of v1, /device:TPU:0, one launch (start us, length us, event | category | flops | bytes accessed | tf_op | source)
XLA Modules:
  0.0 1431.9 jit_solution(1787738146507791716)
XLA Ops:
  37.2 10.6 copy.79
  67.0 72.6 %table.1.table_ref = f32[80,640,640]{2,1,0:T(8,128)} custom-call(f32[640,80,128]{2,1,0:T(8,128)} %broadcast_in_dim.26.ahead_ref, f32[640,80,128]{2,1,0:T(8,128)} %broadcast_in_dim.27.behind_ref, f32[80,640]{1,0:T(8,128)} %get-tuple-element.45.start_ref, f32[1,640]{1,0:T(1,128)} %broadcast_in_dim.32.cos_ref), custom_call_target="tpu_custom_call" | custom-call | tf_op jit(solution)/shard_map/table/pallas_call | solution.py:80
  139.7 49.4 %synthesis.2 = f32[32,80,640]{2,1,0:T(8,128)} custom-call(s32[80]{0:T(128)} %copy-done.24, f32[32,80,640]{2,1,0:T(8,128)} %bitcast.187, f32[80,640,640]{2,1,0:T(8,128)} %table.1.table_ref), custom_call_target="tpu_custom_call" | custom-call | tf_op jit(solution)/shard_map/synthesis/pallas_call | solution.py:155
  189.0 10.1 copy.82
  207.5 14.8 %fusion.47 = (f32[640,1280]{1,0:T(8,128)S(1)}, f32[640,1280]{1,0:T(8,128)}) fusion(s32[640]{0:T(1024)S(1)} %copy-done.23), kind=kLoop, calls=%fused_computation.60 | loop fusion | flops 7372800 | bytes 6556160 | tf_op jit(solution)/shard_map/cos | solution.py:204
  222.3 214.0 %all-to-all-done = f32[2,2,8,80,640]{3,2,1,0,4:T(8,128)} async-done(((f32[2,2,8,80,640]{3,2,1,0,4:T(8,128)}), f32[2,2,8,80,640]{3,2,1,0,4:T(8,128)}, u32[]{:S(2)}, u32[]{:S(2)}) %all-to-all-start) | async-done | bytes 6553632 | tf_op jit(solution)/shard_map/all_to_all | solution.py:236
  436.3 14.0 copy.116
  450.3 10.1 all_to_all.81
  465.8 15.7 %fusion = f32[2,8,80,1280]{3,2,1,0:T(8,128)} fusion(f32[1,8,1280,80]{2,3,1,0:T(8,128)S(1)} %get-tuple-element.47, f32[1,8,1280,80]{2,3,1,0:T(8,128)S(1)} %get-tuple-element.46, f32[640,1280]{1,0:T(8,128)S(1)} %copy-done.4, f32[640,1280]{1,0:T(8,128)S(1)} %get-tuple-element.41), kind=kOutput, calls=%fused_computation.5 | convolution fusion | flops 12586188800 | bytes 19660800 | tf_op jit(solution)/shard_map/flsr,sk->flrk/dot_general | solution.py:243
  481.5 9.6 fusion.27
  495.5 120.3 %all_to_all.108 = f32[2,8,640,80]{3,1,0,2:T(8,128)S(1)} all-to-all(f32[2,8,640,80]{3,1,0,2:T(8,128)} %copy.84), channel_id=1, replica_groups=mesh['lev'=4,'wave'=8] {'wave'}, dimensions={2} | all-to-all | bytes 6553600 | tf_op jit(solution)/shard_map/all_to_all | solution.py:253
  627.0 51.5 %analysis.2 = f32[16,80,640]{2,1,0:T(8,128)} custom-call(s32[80]{0:T(128)} %copy-done.24, f32[16,80,640]{2,1,0:T(8,128)} %broadcast_multiply_fusion.2.fields_ref, f32[80,640,640]{2,1,0:T(8,128)} %table.1.table_ref), custom_call_target="tpu_custom_call" | custom-call | tf_op jit(solution)/shard_map/analysis/pallas_call | solution.py:155
  703.4 10.7 copy.87
  714.1 49.8 %synthesis.3 = f32[32,80,640]{2,1,0:T(8,128)} custom-call(s32[80]{0:T(128)} %copy-done.24, f32[32,80,640]{2,1,0:T(8,128)} %bitcast.189, f32[80,640,640]{2,1,0:T(8,128)} %table.1.table_ref), custom_call_target="tpu_custom_call" | custom-call | tf_op jit(solution)/shard_map/synthesis/pallas_call | solution.py:155
  763.9 10.1 copy.88
  773.9 235.4 %all_to_all.109 = f32[2,2,8,80,640]{3,2,1,0,4:T(8,128)S(1)} all-to-all(f32[2,2,8,80,640]{3,2,1,0,4:T(8,128)} %copy.88), channel_id=1, replica_groups=mesh['lev'=4,'wave'=8] {'wave'}, dimensions={4} | all-to-all | bytes 13107200 | tf_op jit(solution)/shard_map/all_to_all | solution.py:236
  1009.4 9.9 copy.115
  1019.3 10.0 all_to_all.89
  1036.0 16.0 %fusion.4 = f32[2,8,80,1280]{3,2,1,0:T(8,128)} fusion(f32[1,8,1280,80]{2,3,1,0:T(8,128)S(1)} %maximum_bitcast_fusion.3, f32[1,8,1280,80]{2,3,1,0:T(8,128)S(1)} %maximum_bitcast_fusion.2, f32[640,1280]{1,0:T(8,128)S(1)} %copy-done.5, f32[640,1280]{1,0:T(8,128)S(1)} %copy-done.3), kind=kOutput, calls=%fused_computation.9 | convolution fusion | flops 12586188800 | bytes 19660800 | tf_op jit(solution)/shard_map/flsr,sk->flrk/dot_general | solution.py:243
  1052.0 9.6 fusion.24
  1066.2 120.3 %all_to_all.110 = f32[2,8,640,80]{3,1,0,2:T(8,128)S(1)} all-to-all(f32[2,8,640,80]{3,1,0,2:T(8,128)} %copy.90), channel_id=1, replica_groups=mesh['lev'=4,'wave'=8] {'wave'}, dimensions={2} | all-to-all | bytes 6553600 | tf_op jit(solution)/shard_map/all_to_all | solution.py:253
  1197.7 51.5 %analysis.3 = f32[16,80,640]{2,1,0:T(8,128)} custom-call(s32[80]{0:T(128)} %copy-done.24, f32[16,80,640]{2,1,0:T(8,128)} %broadcast_multiply_fusion.1.fields_ref, f32[80,640,640]{2,1,0:T(8,128)} %table.1.table_ref), custom_call_target="tpu_custom_call" | custom-call | tf_op jit(solution)/shard_map/analysis/pallas_call | solution.py:155
  1270.9 56.8 %all-to-all-done.4 = f32[2,8,80,640]{2,1,0,3:T(8,128)} async-done(((f32[2,8,80,640]{2,1,0,3:T(8,128)}), f32[2,8,80,640]{2,1,0,3:T(8,128)}, u32[]{:S(2)}, u32[]{:S(2)}) %all-to-all-start.4) | async-done | bytes 3276832 | tf_op jit(solution)/shard_map/all_to_all | solution.py:264
  1361.4 52.5 %all-to-all-done.5 = f32[2,32,80,160]{3,2,0,1:T(8,128)} async-done(((f32[2,32,80,160]{3,2,0,1:T(8,128)}), f32[2,32,80,160]{3,2,0,1:T(8,128)}, u32[]{:S(2)}, u32[]{:S(2)}) %all-to-all-start.5) | async-done | bytes 3276832 | tf_op jit(solution)/shard_map/all_to_all | solution.py:270
  (122 shorter events, 205.1 us)
Async XLA Ops:
  0.6 1334.2 %copy-start = (f32[32,32]{1,0:T(8,128)S(1)}, f32[32,32]{1,0:T(8,128)}, u32[]{:S(2)}) copy-start(f32[32,32]{1,0:T(8,128)} %param.10) | copy-start | bytes 12292
  1.5 6.0 copy-start.24
  1.7 11.3 copy-start.10
  7.5 5.5 copy-start.1
  18.3 9.1 copy-start.13
  18.3 14.2 slice-start
  18.5 8.9 copy-start.15
  18.5 14.0 slice-start.1
  199.1 8.4 copy-start.23
  199.1 237.2 %all-to-all-start = ((f32[2,2,8,80,640]{3,2,1,0,4:T(8,128)}), f32[2,2,8,80,640]{3,2,1,0,4:T(8,128)}, u32[]{:S(2)}, u32[]{:S(2)}) async-start(f32[2,2,8,80,640]{3,2,1,0,4:T(8,128)} %copy.82), calls=%async_computation | async-start | bytes 20971520 | tf_op jit(solution)/shard_map/all_to_all | solution.py:236
  207.5 252.9 %copy-start.17 = (f32[640]{0:T(1024)}, f32[640]{0:T(1024)S(1)}, u32[]{:S(2)}) copy-start(f32[640]{0:T(1024)S(1)} %get-tuple-element.43) | copy-start | bytes 7684
  207.5 252.9 %copy-start.19 = (f32[640]{0:T(1024)}, f32[640]{0:T(1024)S(1)}, u32[]{:S(2)}) copy-start(f32[640]{0:T(1024)S(1)} %get-tuple-element.44) | copy-start | bytes 7684
  222.3 259.2 %copy-start.2 = (f32[640,1280]{1,0:T(8,128)}, f32[640,1280]{1,0:T(8,128)S(1)}, u32[]{:S(2)}) copy-start(f32[640,1280]{1,0:T(8,128)S(1)} %get-tuple-element.41) | copy-start | bytes 9830404
  465.8 15.7 %copy-start.6 = (f32[8,80,1280]{2,1,0:T(8,128)S(1)}, f32[8,80,1280]{2,1,0:T(8,128)}, u32[]{:S(2)}) copy-start(f32[8,80,1280]{2,1,0:T(8,128)} %param.9) | copy-start | bytes 9830404
  465.8 15.7 %copy-start.8 = (f32[8,80,1280]{2,1,0:T(8,128)S(1)}, f32[8,80,1280]{2,1,0:T(8,128)}, u32[]{:S(2)}) copy-start(f32[8,80,1280]{2,1,0:T(8,128)} %param.8) | copy-start | bytes 9830404
  678.5 5.8 copy-start.11
  1019.3 10.0 copy-start.18
  1019.3 10.0 copy-start.20
  1036.0 16.0 %copy-start.7 = (f32[8,80,1280]{2,1,0:T(8,128)S(1)}, f32[8,80,1280]{2,1,0:T(8,128)}, u32[]{:S(2)}) copy-start(f32[8,80,1280]{2,1,0:T(8,128)} %param.9) | copy-start | bytes 9830404
  1036.0 16.0 %copy-start.9 = (f32[8,80,1280]{2,1,0:T(8,128)S(1)}, f32[8,80,1280]{2,1,0:T(8,128)}, u32[]{:S(2)}) copy-start(f32[8,80,1280]{2,1,0:T(8,128)} %param.8) | copy-start | bytes 9830404
  1249.2 5.7 copy-start.12
  1263.9 6.6 copy-start.26
  1263.9 63.7 %all-to-all-start.4 = ((f32[2,8,80,640]{2,1,0,3:T(8,128)}), f32[2,8,80,640]{2,1,0,3:T(8,128)}, u32[]{:S(2)}, u32[]{:S(2)}) async-start(f32[2,8,80,640]{2,1,0,3:T(8,128)} %multiply_add_fusion), calls=%async_computation.4 | async-start | bytes 10485760 | tf_op jit(solution)/shard_map/all_to_all | solution.py:264
  1350.6 63.3 %all-to-all-start.5 = ((f32[2,32,80,160]{3,2,0,1:T(8,128)}), f32[2,32,80,160]{3,2,0,1:T(8,128)}, u32[]{:S(2)}, u32[]{:S(2)}) async-start(f32[2,32,80,160]{3,2,0,1:T(8,128)} %copy.97), calls=%async_computation.5 | async-start | bytes 10485760 | tf_op jit(solution)/shard_map/all_to_all | solution.py:270
  (8 other events, 26.9 us)
